TPU v7x, 128 devices: a whole 4x4x4 slice. The times are simulated.
128 devices in a mesh: px: 8 (over y, core), py: 16 (over x, z).
Axes of the slice: x: 4, y: 4, z: 4, core: 2. Of those that a mesh axis runs over, the one named last changes fastest.
Arguments:
- parent_field: float32 [192, 384, 640], P('px', 'py'), may hold values from -6 to 6
- nest_field: float32 [192, 384, 640], P('px', 'py'), may hold values from -6 to 6
- anchor: int32 [2], replicated, may hold values from 1 to 125, as said below
- displacement: int32 [2], replicated, may hold values from 1 to 2, as said below
- feedback_weight: float32 [640], replicated, may hold values from 0.3 to 0.9
- rim_weight: float32 [3], replicated, may hold values from 0.3 to 1
Outputs:
- parent_new: float32 [192, 384, 640], P('px', 'py')
- nest_new: float32 [192, 384, 640], P('px', 'py')
Inputs may be any that keep to these rules, and one draw needn't show every extreme that they name: `displacement`: at least one of the two entries equals 2. `anchor`: the two entries differ; one of them equals the largest value.
All inputs are finite; a program needn't handle non-finite values.
Results may differ from a plain program's by a relative error of at most 0.000067.
Values sent between devices are 32-bit elements; how exact they have to be, the bound alone decides.
A program may use at most 128 MiB of HBM per device.

v0:
```python
import jax
import jax.numpy as jnp
from jax import lax
from jax.sharding import PartitionSpec as P

REFINE = 3
MAX_MOVE = 2
RIM_CELLS = 3


def from_behind(value, axis, steps):
    count = lax.axis_size(axis)
    leading, last = (max(0, -steps), min(count, count - steps))
    return lax.ppermute(value, axis, [(source, source + steps) for source in range(leading, last)])


def interp_matrix(rows_total, window_rows):
    row_ids = jnp.arange(rows_total)
    coarse = (row_ids // REFINE)[:, None]
    frac = ((row_ids % REFINE).astype(jnp.float32) + 0.5) / REFINE - 0.5
    frac = frac[:, None]
    columns = jnp.arange(window_rows)[None, :]
    low_side = frac < 0
    weight_left = jnp.where(low_side, -frac, 0.0)
    weight_mid = jnp.where(low_side, 1.0 + frac, 1.0 - frac)
    weight_right = jnp.where(low_side, 0.0, frac)
    result = jnp.where(columns == coarse, weight_left, 0.0)
    result = result + jnp.where(columns == coarse + 1, weight_mid, 0.0)
    result = result + jnp.where(columns == coarse + 2, weight_right, 0.0)
    return result


def rim_blend(distance, rim_weight):
    blend = jnp.zeros(distance.shape, jnp.float32)
    for level in range(RIM_CELLS):
        blend = blend + jnp.where(distance == level, rim_weight[level], 0.0)
    return blend


def local(parent_field, nest_field, anchor, displacement, feedback_weight, rim_weight):
    par_rows, par_cols, chan = parent_field.shape
    nest_rows = nest_field.shape[0]
    nest_cols = nest_field.shape[1]
    count_x = lax.axis_size("px")
    count_y = lax.axis_size("py")
    index_x = lax.axis_index("px")
    index_y = lax.axis_index("py")
    block_x = nest_rows // REFINE
    block_y = nest_cols // REFINE
    window_x = block_x + 2
    window_y = block_y + 2
    shift_x = displacement[0]
    shift_y = displacement[1]
    corner_x = anchor[0] + shift_x
    corner_y = anchor[1] + shift_y
    wanted = jnp.arange(window_x * lax.axis_size("px"))
    global_row = corner_x - 1 + block_x * (wanted // window_x) + wanted % window_x
    local_row = global_row - par_rows * index_x
    inside = (local_row >= 0) & (local_row < par_rows)
    picked = jnp.take(parent_field, jnp.clip(local_row, 0, par_rows - 1), axis=0)
    band = lax.psum_scatter(
        jnp.where(inside[:, None, None], picked, 0.0), "px", scatter_dimension=0, tiled=True
    )
    wanted = jnp.arange(window_y * lax.axis_size("py"))
    global_col = corner_y - 1 + block_y * (wanted // window_y) + wanted % window_y
    local_col = global_col - par_cols * index_y
    inside = (local_col >= 0) & (local_col < par_cols)
    picked = jnp.take(band, jnp.clip(local_col, 0, par_cols - 1), axis=1)
    picked = jnp.where(inside[None, :, None], picked, 0.0)
    window = lax.psum_scatter(jnp.swapaxes(picked, 0, 1), "py", scatter_dimension=0, tiled=True)
    weights_x = interp_matrix(nest_rows, window_x)
    weights_y = interp_matrix(nest_cols, window_y)
    inner_sum = jnp.einsum("jy,yxc->xjc", weights_y, window, precision=lax.Precision.HIGHEST)
    interp = jnp.einsum("ix,xjc->ijc", weights_x, inner_sum, precision=lax.Precision.HIGHEST)
    margin = REFINE * MAX_MOVE
    below = from_behind(nest_field[:margin], "px", -1)
    taller = jnp.concatenate([nest_field, below], axis=0)
    beside = from_behind(taller[:, :margin], "py", -1)
    wider = jnp.concatenate([taller, beside], axis=1)
    shifted = lax.dynamic_slice(
        wider, (REFINE * shift_x, REFINE * shift_y, jnp.int32(0)), nest_field.shape
    )
    nest_nx = nest_rows * count_x
    nest_ny = nest_cols * count_y
    rows_global = nest_rows * index_x + jnp.arange(nest_rows)[:, None, None]
    cols_global = nest_cols * index_y + jnp.arange(nest_cols)[None, :, None]
    newly_entered = (rows_global + REFINE * shift_x >= nest_nx) | (
        cols_global + REFINE * shift_y >= nest_ny
    )
    moved = jnp.where(newly_entered, interp, shifted)
    distance = jnp.minimum(
        jnp.minimum(rows_global, cols_global),
        jnp.minimum(nest_nx - 1 - rows_global, nest_ny - 1 - cols_global),
    )
    blend = rim_blend(distance, rim_weight)
    nest_new = moved + blend * (interp - moved)
    average = nest_new.reshape(block_x, REFINE, block_y, REFINE, chan).sum(axis=(1, 3)) * (
        1.0 / (REFINE * REFINE)
    )
    relative_x = par_rows * index_x + jnp.arange(par_rows) - corner_x
    relative_y = par_cols * index_y + jnp.arange(par_cols) - corner_y
    within_x = (relative_x >= 0) & (relative_x < block_x * count_x)
    within_y = (relative_y >= 0) & (relative_y < block_y * count_y)
    source_x = relative_x // block_x
    source_y = relative_y // block_y
    offset_x = relative_x % block_x
    offset_y = relative_y % block_y
    shards = lax.all_gather(average[None], ("px", "py"), axis=0, tiled=True)
    members = shards.shape[0]
    member = source_x[:, None] * count_y + source_y[None, :]
    valid = within_x[:, None] & within_y[None, :] & (member >= 0) & (member < members)
    flat_index = (
        jnp.clip(member, 0, members - 1) * (block_x * block_y)
        + offset_x[:, None] * block_y
        + offset_y[None, :]
    )
    flat_rows = shards.reshape(members * block_x * block_y, chan)
    picked = jnp.take(flat_rows, flat_index.reshape(-1), axis=0).reshape(par_rows, par_cols, chan)
    summed = jnp.where(valid[:, :, None], picked, 0.0)
    covered = (within_x[:, None] & within_y[None, :])[:, :, None]
    parent_new = jnp.where(
        covered, parent_field + feedback_weight * (summed - parent_field), parent_field
    )
    return (parent_new, nest_new)


def solution(mesh):
    in_specs = (P("px", "py", None), P("px", "py", None), P(), P(), P(), P())
    out_specs = (P("px", "py", None), P("px", "py", None))
    return jax.shard_map(local, mesh=mesh, in_specs=in_specs, out_specs=out_specs, check_vma=False)
```

profile of v0, /device:TPU:1, one launch (start us, length us, event | category | flops | bytes accessed | tf_op | source)
XLA Modules:
  0.0 271.6 jit_solution(3452023540534348857)
XLA Ops:
  7.2 1.3 fusion.59
  8.5 1.3 fusion.58
  11.3 4.5 %gather_fusion = f32[80,24,640]{2,1,0:T(8,128)} fusion(f32[24,24,640]{2,1,0:T(8,128)} %param.6, s32[1024]{0:T(1024)S(1)} %pad_clamp_fusion.2), kind=kCustom, calls=%fused_computation | custom fusion | bytes 9830720 | tf_op jit(solution)/shard_map/jit(_take)/gather | solution.py:60
  15.7 5.2 %select_select_fusion.1 = f32[80,24,640]{2,1,0:T(8,128)} fusion(f32[80,24,640]{2,1,0:T(8,128)} %gather_fusion, pred[80]{0:T(512)(128)(4,1)S(1)} %get-tuple-element.20, pred[80]{0:T(512)(128)(4,1)S(1)} %get-tuple-element.21), kind=kLoop, calls=%fused_computation.4 | loop fusion | flops 2457600 | bytes 9830560 | tf_op jit(solution)/shard_map/jit(_where)/select_n | solution.py:62
  22.3 38.7 %reduce-scatter.3.cloned.1.call-done = f32[10,24,640]{2,1,0:T(8,128)} async-done(((f32[80,24,640]{2,1,0:T(8,128)}), f32[10,24,640]{2,1,0:T(8,128)}) %reduce-scatter.3.cloned.1.call-update) | async-done | bytes 614416 | tf_op jit(solution)/shard_map/reduce_scatter | solution.py:61
  61.0 1.2 copy.27
  62.2 3.7 %gather_fusion.1 = f32[160,10,640]{2,1,0:T(8,128)} fusion(f32[10,24,640]{2,0,1:T(8,128)S(1)} %copy.27, s32[1024]{0:T(1024)S(1)} %pad_clamp_fusion.1), kind=kCustom, calls=%fused_computation.1 | custom fusion | bytes 8192640 | tf_op jit(solution)/shard_map/jit(_take)/gather | solution.py:68
  65.9 5.3 %select_select_fusion = f32[160,10,640]{2,1,0:T(8,128)} fusion(f32[160,10,640]{2,1,0:T(8,128)} %gather_fusion.1, pred[160]{0:T(512)(128)(4,1)S(1)} %get-tuple-element.33, pred[160]{0:T(512)(128)(4,1)S(1)} %get-tuple-element.32), kind=kLoop, calls=%fused_computation.3 | loop fusion | flops 2048000 | bytes 8192320 | tf_op jit(solution)/shard_map/jit(_where)/select_n | solution.py:69
  71.3 0.9 slice-done
  72.3 5.3 %collective-permute-start = (f32[6,24,640]{2,0,1:T(8,128)S(1)}, f32[6,24,640]{2,0,1:T(8,128)S(1)}, u32[]{:S(2)}, u32[]{:S(2)}) collective-permute-start(f32[6,24,640]{2,0,1:T(8,128)S(1)} %copy.40), channel_id=1, source_target_pairs={{16,0},{32,16},{48,32},{64,48},{80,64},{96,80},{112,96},{17,1},{33... | collective-permute-start | bytes 1105928 | tf_op jit(solution)/shard_map/ppermute | solution.py:14
  78.9 0.7 fusion.57
  79.6 2.0 select_add_fusion
  81.7 1.8 constant_dynamic-update-slice_fusion.1
  83.7 1.3 collective-permute-start.1
  85.0 72.3 %reduce-scatter.5.cloned.1.call-done = f32[10,10,640]{2,1,0:T(8,128)} async-done(((f32[160,10,640]{2,1,0:T(8,128)}), f32[10,10,640]{2,1,0:T(8,128)}) %reduce-scatter.5.cloned.1.call-update) | async-done | bytes 256016 | tf_op jit(solution)/shard_map/reduce_scatter | solution.py:70
  157.3 1.7 convolution_bitcast_fusion
  159.0 1.9 multiply_add_fusion
  161.3 0.7 reshape.659
  162.0 0.4 copy-done.1
  162.4 1.3 reduce_sum.9
  163.7 1.6 broadcast_multiply_fusion
  165.7 87.6 %all-gather.3.cloned.1.call-done = f32[1024,8,640]{2,1,0:T(8,128)} async-done(((f32[8,8,640]{2,1,0:T(8,128)}), f32[1024,8,640]{2,1,0:T(8,128)}) %all-gather.3.cloned.1.call-update) | async-done | bytes 20971536 | tf_op jit(solution)/shard_map/all_gather | solution.py:108
  253.3 10.1 %gather_fusion.2 = f32[576,640]{1,0:T(8,128)S(1)} fusion(f32[8192,640]{1,0:T(8,128)} %bitcast.19, s32[1024]{0:T(1024)S(1)} %pad_clamp_fusion), kind=kCustom, calls=%fused_computation.2 | custom fusion | bytes 2951424 | tf_op jit(solution)/shard_map/jit(_take)/gather | solution.py:118
  263.5 1.5 add_select_fusion
  (44 shorter events, 1.3 us)
Async XLA Ops:
  7.2 53.8 %reduce-scatter.3.cloned.1.call-start = ((), (), s32[]{:S(2)}) async-start(), calls=%async_computation.2 | async-start | bytes 5529600 | tf_op jit(solution)/shard_map/reduce_scatter | solution.py:61
  20.9 136.4 %reduce-scatter.5.cloned.1.call-start = ((), (), s32[]{:S(2)}) async-start(), calls=%async_computation.3 | async-start | bytes 6963200 | tf_op jit(solution)/shard_map/reduce_scatter | solution.py:70
  71.2 1.0 slice-start
  71.2 7.7 %copy-start.2 = (f32[3]{0:T(128)S(1)}, f32[3]{0:T(128)}, u32[]{:S(2)}) copy-start(f32[3]{0:T(128)} %param.11) | copy-start | bytes 40
  71.2 182.1 %all-gather.3.cloned.1.call-start = ((), (), s32[]{:S(2)}) async-start(), calls=%async_computation.4 | async-start | bytes 21135360 | tf_op jit(solution)/shard_map/all_gather | solution.py:108
  72.3 11.3 %collective-permute-start = (f32[6,24,640]{2,0,1:T(8,128)S(1)}, f32[6,24,640]{2,0,1:T(8,128)S(1)}, u32[]{:S(2)}, u32[]{:S(2)}) collective-permute-start(f32[6,24,640]{2,0,1:T(8,128)S(1)} %copy.40), channel_id=1, source_target_pairs={{16,0},{32,16},{48,32},{64,48},{80,64},{96,80},{112,96},{17,1},{33... | collective-permute-start | bytes 1105928 | tf_op jit(solution)/shard_map/ppermute | solution.py:14
  83.7 75.3 %collective-permute-start.1 = (f32[30,6,640]{2,0,1:T(8,128)S(1)}, f32[30,6,640]{2,0,1:T(8,128)S(1)}, u32[]{:S(2)}, u32[]{:S(2)}) collective-permute-start(f32[30,6,640]{2,0,1:T(8,128)S(1)} %slice.43), channel_id=1, source_target_pairs={{1,0},{2,1},{3,2},{4,3},{5,4},{6,5},{7,6},{8,7},{9,8},{10,9},{11,1... | collective-permute-start | bytes 1382408 | tf_op jit(solution)/shard_map/ppermute | solution.py:14
  161.3 1.1 copy-start.1
  253.3 10.2 %copy-start = (f32[24,24,640]{2,1,0:T(8,128)S(1)}, f32[24,24,640]{2,1,0:T(8,128)}, u32[]{:S(2)}) copy-start(f32[24,24,640]{2,1,0:T(8,128)} %param.6) | copy-start | bytes 4423684
  253.3 10.2 %copy-start.3 = (f32[640]{0:T(1024)S(1)}, f32[640]{0:T(1024)}, u32[]{:S(2)}) copy-start(f32[640]{0:T(1024)} %param.10) | copy-start | bytes 7684
Sparse Core Ops, SparseCore 0:
  21.0 39.9 reduce-scatter.2
  71.3 85.9 reduce-scatter.4
  165.5 87.8 all-gather.2
where the time goes:
time: 272 us
  waiting for transfers between devices  199 us (73%)
  local copies, waits for them, and re-layouts  27.3 us (10%)
  between operations  17.9 us (7%)
  other arithmetic  17.4 us (6%)
  starting transfers between devices  6.69 us (2%)
  matrix products  3.63 us (1%)
    all_gather x1, waiting for transfers between devices, local(): shards = lax.all_gather(average[None], ('px', 'py'), axis=0, tiled=True)  87.6 us
    reduce_scatter x1, waiting for transfers between devices, local(): lax.psum_scatter(jnp.swapaxes(picked, 0, 1), 'py', scatter_dimension=0, t...  72.3 us
    reduce_scatter x1, waiting for transfers between devices, local(): lax.psum_scatter(jnp.where(inside[:, None, None], picked, 0.0), 'px', sca...  38.7 us
    gather x1, local copies, waits for them, and re-layouts, local(): jnp.take(flat_rows, flat_index.reshape(-1), axis=0)  10.1 us
    ppermute x2, starting transfers between devices, from_behind(): lax.ppermute(value, axis, [(source, source + steps) for source in range(l...  6.57 us
  transfers between devices with their start and end apart: 5, of which 3 were waited for; matrix products, arithmetic and copies ran while one was open for 3% of the time, Pallas kernels for 0%

commit v1 on v0

--- a/solution.py
+++ b/solution.py
@@ -1,3 +1,4 @@
+import functools
 import jax
 import jax.numpy as jnp
 from jax import lax
@@ -6,6 +7,16 @@
 REFINE = 3
 MAX_MOVE = 2
 RIM_CELLS = 3
+
+
+def _convert_group(my_tile, at_axis):
+    e_now = jnp.stack([my_tile for _ in range(lax.axis_size(("px", "py")))], 0)
+    upper = lax.all_to_all(e_now, axis_name=("px", "py"), split_axis=0, concat_axis=0)
+    heard = jnp.concatenate(upper, at_axis)
+    return heard
+
+
+_work_outputs = functools.partial(_convert_group, at_axis=0)
 
 
 def from_behind(value, axis, steps):
@@ -105,7 +116,7 @@
     source_y = relative_y // block_y
     offset_x = relative_x % block_x
     offset_y = relative_y % block_y
-    shards = lax.all_gather(average[None], ("px", "py"), axis=0, tiled=True)
+    shards = _work_outputs(average[None])
     members = shards.shape[0]
     member = source_x[:, None] * count_y + source_y[None, :]
     valid = within_x[:, None] & within_y[None, :] & (member >= 0) & (member < members)

time: 272 us -> 508 us (1.87); the launches traced: 272 us -> 500 us
  waiting for transfers between devices: 199 us -> 408 us
  starting transfers between devices: 6.69 us -> 16.4 us
  local copies, waits for them, and re-layouts: 27.3 us -> 37 us
    all_to_all x0 -> x1, waiting for transfers between devices: none -> 298 us  [_convert_group(): lax.all_to_all(e_now, axis_name=('px', 'py'), split_axis=0, concat_axis=0)]
    all_gather x1 -> x0, waiting for transfers between devices: 87.6 us -> none  [local(): shards = lax.all_gather(average[None], ('px', 'py'), axis=0, tiled=True)]
    all_to_all x0 -> x1, starting transfers between devices: none -> 9.71 us  [_convert_group(): lax.all_to_all(e_now, axis_name=('px', 'py'), split_axis=0, concat_axis=0)]
    another operation x0 -> x1, local copies, waits for them, and re-layouts: none -> 9.59 us  [_convert_group(): e_now = jnp.stack([my_tile for _ in range(lax.axis_size(('px', 'py')))], 0)]
  transfers between devices with their start and end apart: 5 -> 5, of which waited for: 3 -> 3; matrix products, arithmetic and copies ran while one was open for 3% -> 1% of each run, Pallas kernels for 0% -> 0%
where the time goes in v1:
time: 508 us; the launch traced here: 500 us
  waiting for transfers between devices  408 us (80%)
  local copies, waits for them, and re-layouts  37 us (7%)
  between operations  18.1 us (4%)
  other arithmetic  16.7 us (3%)
  starting transfers between devices  16.4 us (3%)
    all_to_all x1, waiting for transfers between devices, _convert_group(): lax.all_to_all(e_now, axis_name=('px', 'py'), split_axis=0, concat_axis=0)  298 us
    reduce_scatter x1, waiting for transfers between devices, local(): lax.psum_scatter(jnp.swapaxes(picked, 0, 1), 'py', scatter_dimension=0, t...  72.1 us
    reduce_scatter x1, waiting for transfers between devices, local(): lax.psum_scatter(jnp.where(inside[:, None, None], picked, 0.0), 'px', sca...  38.7 us
  transfers between devices with their start and end apart: 5, of which 3 were waited for; matrix products, arithmetic and copies ran while one was open for 1% of the time, Pallas kernels for 0%

profile of v1, /device:TPU:1, one launch (start us, length us, event | category | flops | bytes accessed | tf_op | source)
XLA Modules:
  0.0 500.2 jit_solution(12691112207759947965)
XLA Ops:
  7.2 1.3 fusion.59
  8.5 1.4 fusion.58
  11.2 4.4 gather_fusion
  15.6 5.2 %select_select_fusion.1 = f32[80,24,640]{2,1,0:T(8,128)} fusion(f32[80,24,640]{2,1,0:T(8,128)} %gather_fusion, pred[80]{0:T(512)(128)(4,1)S(1)} %get-tuple-element.20, pred[80]{0:T(512)(128)(4,1)S(1)} %get-tuple-element.21), kind=kLoop, calls=%fused_computation.4 | loop fusion | flops 2457600 | bytes 9830560 | tf_op jit(solution)/shard_map/jit(_where)/select_n | solution.py:73
  22.2 38.7 %reduce-scatter.3.cloned.1.call-done = f32[10,24,640]{2,1,0:T(8,128)} async-done(((f32[80,24,640]{2,1,0:T(8,128)}), f32[10,24,640]{2,1,0:T(8,128)}) %reduce-scatter.3.cloned.1.call-update) | async-done | bytes 614416 | tf_op jit(solution)/shard_map/reduce_scatter | solution.py:72
  60.9 1.2 copy.27
  62.1 3.7 gather_fusion.1
  65.8 5.3 %select_select_fusion = f32[160,10,640]{2,1,0:T(8,128)} fusion(f32[160,10,640]{2,1,0:T(8,128)} %gather_fusion.1, pred[160]{0:T(512)(128)(4,1)S(1)} %get-tuple-element.33, pred[160]{0:T(512)(128)(4,1)S(1)} %get-tuple-element.32), kind=kLoop, calls=%fused_computation.3 | loop fusion | flops 2048000 | bytes 8192320 | tf_op jit(solution)/shard_map/jit(_where)/select_n | solution.py:80
  71.1 1.0 slice-done
  72.2 5.3 %collective-permute-start = (f32[6,24,640]{2,0,1:T(8,128)S(1)}, f32[6,24,640]{2,0,1:T(8,128)S(1)}, u32[]{:S(2)}, u32[]{:S(2)}) collective-permute-start(f32[6,24,640]{2,0,1:T(8,128)S(1)} %copy.40), channel_id=1, source_target_pairs={{16,0},{32,16},{48,32},{64,48},{80,64},{96,80},{112,96},{17,1},{33... | collective-permute-start | bytes 1105928 | tf_op jit(solution)/shard_map/ppermute | solution.py:25
  79.4 2.0 select_add_fusion
  81.6 1.8 constant_dynamic-update-slice_fusion.1
  83.6 1.3 collective-permute-start.1
  84.9 72.1 %reduce-scatter.5.cloned.1.call-done = f32[10,10,640]{2,1,0:T(8,128)} async-done(((f32[160,10,640]{2,1,0:T(8,128)}), f32[10,10,640]{2,1,0:T(8,128)}) %reduce-scatter.5.cloned.1.call-update) | async-done | bytes 256016 | tf_op jit(solution)/shard_map/reduce_scatter | solution.py:81
  157.1 1.7 convolution_bitcast_fusion
  158.8 1.9 multiply_add_fusion
  161.0 0.7 reshape.653
  162.1 1.3 reduce_sum.9
  163.5 0.9 broadcast_multiply_fusion
  164.4 9.6 %stack.3 = f32[128,1,8,8,640]{4,3,2,1,0:T(8,128)} broadcast(f32[8,8,640]{2,1,0:T(8,128)S(1)} %broadcast_multiply_fusion), dimensions={2,3,4} | broadcast | bytes 21135360 | tf_op jit(solution)/shard_map/stack | solution.py:13
  174.0 9.7 %all-to-all-start = ((f32[128,1,8,8,640]{4,3,2,1,0:T(8,128)}), f32[128,1,8,8,640]{4,3,2,1,0:T(8,128)}, u32[]{:S(2)}, u32[]{:S(2)}) async-start(f32[128,1,8,8,640]{4,3,2,1,0:T(8,128)} %stack.3), calls=%async_computation.2 | async-start | bytes 41943040 | tf_op jit(solution)/shard_map/all_to_all | solution.py:14
  184.1 297.6 %all-to-all-done = f32[128,1,8,8,640]{4,3,2,1,0:T(8,128)} async-done(((f32[128,1,8,8,640]{4,3,2,1,0:T(8,128)}), f32[128,1,8,8,640]{4,3,2,1,0:T(8,128)}, u32[]{:S(2)}, u32[]{:S(2)}) %all-to-all-start) | async-done | bytes 20971552 | tf_op jit(solution)/shard_map/all_to_all | solution.py:14
  481.7 10.1 %gather_fusion.2 = f32[576,640]{1,0:T(8,128)S(1)} fusion(f32[8192,640]{1,0:T(8,128)} %bitcast.11, s32[1024]{0:T(1024)S(1)} %pad_clamp_fusion), kind=kCustom, calls=%fused_computation.2 | custom fusion | bytes 2951424 | tf_op jit(solution)/shard_map/jit(_take)/gather | solution.py:129
  491.8 1.5 add_select_fusion
  (44 shorter events, 2.3 us)
Async XLA Ops:
  7.2 53.7 %reduce-scatter.3.cloned.1.call-start = ((), (), s32[]{:S(2)}) async-start(), calls=%async_computation.3 | async-start | bytes 5529600 | tf_op jit(solution)/shard_map/reduce_scatter | solution.py:72
  20.8 136.3 %reduce-scatter.5.cloned.1.call-start = ((), (), s32[]{:S(2)}) async-start(), calls=%async_computation.4 | async-start | bytes 6963200 | tf_op jit(solution)/shard_map/reduce_scatter | solution.py:81
  71.1 1.0 slice-start
  71.1 7.7 %copy-start.2 = (f32[3]{0:T(128)S(1)}, f32[3]{0:T(128)}, u32[]{:S(2)}) copy-start(f32[3]{0:T(128)} %param.11) | copy-start | bytes 40
  72.2 11.3 %collective-permute-start = (f32[6,24,640]{2,0,1:T(8,128)S(1)}, f32[6,24,640]{2,0,1:T(8,128)S(1)}, u32[]{:S(2)}, u32[]{:S(2)}) collective-permute-start(f32[6,24,640]{2,0,1:T(8,128)S(1)} %copy.40), channel_id=1, source_target_pairs={{16,0},{32,16},{48,32},{64,48},{80,64},{96,80},{112,96},{17,1},{33... | collective-permute-start | bytes 1105928 | tf_op jit(solution)/shard_map/ppermute | solution.py:25
  83.6 75.2 %collective-permute-start.1 = (f32[30,6,640]{2,0,1:T(8,128)S(1)}, f32[30,6,640]{2,0,1:T(8,128)S(1)}, u32[]{:S(2)}, u32[]{:S(2)}) collective-permute-start(f32[30,6,640]{2,0,1:T(8,128)S(1)} %slice.43), channel_id=1, source_target_pairs={{1,0},{2,1},{3,2},{4,3},{5,4},{6,5},{7,6},{8,7},{9,8},{10,9},{11,1... | collective-permute-start | bytes 1382408 | tf_op jit(solution)/shard_map/ppermute | solution.py:25
  161.0 1.1 copy-start.1
  174.0 307.6 %all-to-all-start = ((f32[128,1,8,8,640]{4,3,2,1,0:T(8,128)}), f32[128,1,8,8,640]{4,3,2,1,0:T(8,128)}, u32[]{:S(2)}, u32[]{:S(2)}) async-start(f32[128,1,8,8,640]{4,3,2,1,0:T(8,128)} %stack.3), calls=%async_computation.2 | async-start | bytes 41943040 | tf_op jit(solution)/shard_map/all_to_all | solution.py:14
  481.7 10.2 %copy-start = (f32[24,24,640]{2,1,0:T(8,128)S(1)}, f32[24,24,640]{2,1,0:T(8,128)}, u32[]{:S(2)}) copy-start(f32[24,24,640]{2,1,0:T(8,128)} %param.6) | copy-start | bytes 4423684
  481.7 10.2 %copy-start.3 = (f32[640]{0:T(1024)S(1)}, f32[640]{0:T(1024)}, u32[]{:S(2)}) copy-start(f32[640]{0:T(1024)} %param.10) | copy-start | bytes 7684
Sparse Core Ops, SparseCore 0:
  20.9 39.9 reduce-scatter.2
  71.2 85.7 reduce-scatter.4
